TPU v7x, 128 devices: a whole 4x4x4 slice. The times are simulated.
128 devices in a mesh: row: 8 (over z, core), col: 8 (over y_hi, x), freq: 2 (over y_lo).
Axes of the slice: x: 4, y: 4 (y_hi: 2, y_lo: 2; y = y_hi * 2 + y_lo), z: 4, core: 2. Of those that a mesh axis runs over, the one named last changes fastest.
Arguments:
- pair_elements: bfloat16 [2, 1024, 8192], P(None, ('row', 'freq'), 'col'), may hold values from -1.59375 to 1.59375
- transitions: int32 [3, 1024], replicated, may hold values from 0 to 63, as said below
- energies: float32 [16, 64], replicated, may hold values from -3 to 3
- occupations: int32 [16, 64], replicated, may hold values from 0 to 2
- frequencies: float32 [4], P('freq'), may hold values from 0.2 to 2
Outputs:
- chi_zero: float32 [4, 2, 8192, 8192], P('freq', None, 'row', 'col')
Inputs may be any that keep to these rules, and one draw needn't show every extreme that they name: transitions[0] is a k-point below 16, transitions[1] a valence band below 32, transitions[2] a conduction band of 32 to 63.
All inputs are finite; a program needn't handle non-finite values.
Results may differ from a plain program's by a relative error of at most 0.0028.
Values may be sent and summed in bfloat16 or wider, within the bound.
A program may use at most 128 MiB of HBM per device.

v0:
```python
import jax
import jax.numpy as jnp
from jax import lax
from jax.sharding import PartitionSpec as P


def broadcast(value, axis, source):
    kept = jnp.where(lax.axis_index(axis) == source, value, 0).astype(value.dtype)
    return lax.psum(kept, axis)


def lookup(table, flat_rows):
    flat = table.reshape(-1)
    onehot = (flat_rows[:, None] == jnp.arange(flat.shape[0], dtype=jnp.int32)[None, :]).astype(
        jnp.float32
    )
    return jnp.dot(onehot, flat, precision=lax.Precision.HIGHEST)


def weights(transitions, energies, occupations, frequencies):
    bands = energies.shape[1]
    kpoint = transitions[0]
    valence_rows = kpoint * bands + transitions[1]
    conduction_rows = kpoint * bands + transitions[2]
    gap = lookup(energies, conduction_rows) - lookup(energies, valence_rows)
    occ_float = occupations.astype(jnp.float32)
    filled = lookup(occ_float, valence_rows) - lookup(occ_float, conduction_rows)
    return (
        filled[None, :]
        * 2.0
        * gap[None, :]
        / (gap[None, :] * gap[None, :] + frequencies[:, None] * frequencies[:, None])
    )


def contribute(left, right, weight_block):
    right_both = jnp.concatenate([right[0], right[1]], 0)
    dims = (((0,), (0,)), ((), ()))
    results = []
    for index in range(weight_block.shape[0]):
        scaled = (left.astype(jnp.float32) * weight_block[index][None, :, None]).astype(
            jnp.bfloat16
        )
        real_left = jnp.concatenate([scaled[0], scaled[1]], 0)
        imag_left = jnp.concatenate([scaled[1], -scaled[0]], 0)
        real_component = lax.dot_general(
            real_left, right_both, dims, preferred_element_type=jnp.float32
        )
        imag_part = lax.dot_general(imag_left, right_both, dims, preferred_element_type=jnp.float32)
        results.append(jnp.stack([real_component, imag_part], 0))
    return jnp.stack(results, 0)


def body(pair_elements, transitions, energies, occupations, frequencies):
    weight = weights(transitions, energies, occupations, frequencies)
    column_panel = lax.all_gather(pair_elements, ("row", "freq"), axis=1, tiled=True)
    row_panel = broadcast(column_panel, "col", lax.axis_index("row"))
    chi_zero = contribute(row_panel, column_panel, weight)
    return chi_zero


def solution(mesh):
    in_specs = (P(None, ("row", "freq"), "col"), P(), P(), P(), P("freq"))
    out_specs = P("freq", None, "row", "col")
    return jax.shard_map(body, mesh=mesh, in_specs=in_specs, out_specs=out_specs, check_vma=False)
```

profile of v0, /device:TPU:0, one launch (start us, length us, event | category | flops | bytes accessed | tf_op | source)
XLA Modules:
  0.0 220.7 jit_solution(16224956101808167653)
XLA Ops:
  6.5 0.0 all-gather.2.cloned.1.call-start
  6.5 0.7 all-gather.2.cloned.1.call-update
  7.3 0.0 all-reduce.2.cloned.1.call-start
  7.3 53.0 %all-gather.2.cloned.1.call-done = bf16[2,1024,1024]{2,1,0:T(8,128)(2,1)} async-done(((bf16[2,64,1024]{2,1,0:T(8,128)(2,1)}), bf16[2,1024,1024]{2,1,0:T(8,128)(2,1)}) %all-gather.2.cloned.1.call-update) | async-done | bytes 4194320 | tf_op jit(solution)/shard_map/all_gather | solution.py:56
  60.4 4.5 %broadcast_select_fusion = bf16[2,1024,1024]{2,1,0:T(8,128)(2,1)} fusion(bf16[2,1024,1024]{2,1,0:T(8,128)(2,1)} %all-gather.2.cloned.1.call-done, pred[]{:T(512)S(6)} %eq.14), kind=kLoop, calls=%fused_computation.30 | loop fusion | flops 2097152 | bytes 8388609 | tf_op jit(solution)/shard_map/jit(_where)/select_n | solution.py:8
  64.8 0.0 copy-start.5
  64.8 0.0 copy-start.3
  64.8 0.0 copy-start.4
  64.8 0.0 copy-start.2
  64.8 0.0 all-reduce.2.cloned.1.call-update
  64.9 0.6 copy-done.5
  65.5 0.1 copy-done.3
  65.5 0.1 reshape.45
  65.6 0.0 copy-done.4
  65.6 0.1 reshape.41
  65.7 0.0 copy-done.2
  65.7 0.0 copy-start
  65.7 2.0 fusion.18
  67.7 2.0 fusion.19
  69.7 2.0 fusion.21
  71.7 2.0 fusion.20
  73.8 0.1 add_divide_fusion
  73.9 0.0 copy-done
  73.9 1.8 slice_bitcast_fusion.3
  75.7 101.0 %all-reduce.2.cloned.1.call-done = bf16[2,1024,1024]{2,1,0:T(8,128)(2,1)} async-done(((bf16[2,1024,1024]{2,1,0:T(8,128)(2,1)}), bf16[2,1024,1024]{2,1,0:T(8,128)(2,1)}) %all-reduce.2.cloned.1.call-update) | async-done | bytes 4194320 | tf_op jit(solution)/shard_map/psum | solution.py:9
  176.6 2.9 %fusion = (bf16[2,1024,1024]{2,1,0:T(8,128)(2,1)S(1)}, bf16[2,1024,1024]{2,1,0:T(8,128)(2,1)S(1)}) fusion(bf16[2,1024,1024]{2,1,0:T(8,128)(2,1)} %all-reduce.2.cloned.1.call-done, f32[1024]{0:T(1024)S(1)} %bitcast.40, f32[1024]{0:T(1024)S(1)} %bitcast.41), kind=kLoop, calls=%fused_computation.3 | loop fusion | flops 10485760 | bytes 12591104 | tf_op jit(solution)/shard_map/convert_element_type | solution.py:41
  179.6 0.3 fusion.42
  179.9 0.0 copy-start.1
  179.9 1.1 slice_bitcast_fusion.1
  181.0 0.4 copy-done.1
  181.5 4.7 %fusion.25 = f32[1,1024,1024]{2,1,0:T(8,128)S(1)} fusion(bf16[1024,1024]{1,0:T(8,128)(2,1)S(1)} %get-tuple-element.10, bf16[1024,1024]{1,0:T(8,128)(2,1)S(1)} %get-tuple-element.9, bf16[1024,1024]{1,0:T(8,128)(2,1)S(1)} %copy-done.1, bf16[1024,1024]{1,0:T(8,128)(2,1)S(1)} %get-tuple-element.11), kind=kOutput, calls=%fused_computation.32 | convolution fusion | flops 4311744512 | bytes 12582912 | tf_op jit(solution)/shard_map/dot_general | solution.py:46
  186.1 4.7 %fusion.22 = f32[1,1024,1024]{2,1,0:T(8,128)S(1)} fusion(bf16[1024,1024]{1,0:T(8,128)(2,1)S(1)} %get-tuple-element.22, bf16[1024,1024]{1,0:T(8,128)(2,1)S(1)} %get-tuple-element.10, bf16[1024,1024]{1,0:T(8,128)(2,1)S(1)} %copy-done.1, bf16[1024,1024]{1,0:T(8,128)(2,1)S(1)} %get-tuple-element.11), kind=kOutput, calls=%fused_computation.31 | convolution fusion | flops 4311744512 | bytes 12582912 | tf_op jit(solution)/shard_map/dot_general | solution.py:49
  190.8 4.9 %fusion.31 = f32[1,1024,1024]{2,1,0:T(8,128)S(1)} fusion(bf16[1024,1024]{1,0:T(8,128)(2,1)S(1)} %get-tuple-element.19, bf16[1024,1024]{1,0:T(8,128)(2,1)S(1)} %get-tuple-element.20, bf16[1024,1024]{1,0:T(8,128)(2,1)S(1)} %copy-done.1, bf16[1024,1024]{1,0:T(8,128)(2,1)S(1)} %get-tuple-element.11), kind=kOutput, calls=%fused_computation.34 | convolution fusion | flops 4311744512 | bytes 12582912 | tf_op jit(solution)/shard_map/dot_general | solution.py:46
  195.7 6.8 %fusion.28 = f32[1,1024,1024]{2,1,0:T(8,128)} fusion(bf16[1024,1024]{1,0:T(8,128)(2,1)S(1)} %get-tuple-element.21, bf16[1024,1024]{1,0:T(8,128)(2,1)S(1)} %get-tuple-element.19, bf16[1024,1024]{1,0:T(8,128)(2,1)S(1)} %copy-done.1, bf16[1024,1024]{1,0:T(8,128)(2,1)S(1)} %get-tuple-element.11), kind=kOutput, calls=%fused_computation.33 | convolution fusion | flops 4311744512 | bytes 12582912 | tf_op jit(solution)/shard_map/dot_general | solution.py:49
  202.5 1.7 maximum_bitcast_fusion.1
  204.1 3.4 %maximum_bitcast_fusion = f32[1,2,1024,1024]{3,2,1,0:T(8,128)S(1)} fusion(f32[1,1024,1024]{2,1,0:T(8,128)} %fusion.28, f32[1,1024,1024]{2,1,0:T(8,128)S(1)} %fusion.31), kind=kLoop, calls=%fused_computation.5 | loop fusion | flops 2097152 | bytes 16777216 | tf_op jit(solution)/shard_map/stack | solution.py:51
  207.6 6.2 %pad_maximum_fusion = f32[2,2,1024,1024]{3,2,1,0:T(8,128)} fusion(f32[1,2,1024,1024]{3,2,1,0:T(8,128)S(1)} %maximum_bitcast_fusion.1, f32[1,2,1024,1024]{3,2,1,0:T(8,128)S(1)} %maximum_bitcast_fusion), kind=kLoop, calls=%fused_computation | loop fusion | flops 4194304 | bytes 33554432 | tf_op jit(solution)/shard_map/stack | solution.py:51
  (5 shorter events, 0.0 us)
Async XLA Ops:
  6.5 53.8 %all-gather.2.cloned.1.call-start = ((), (), s32[]{:S(2)}) async-start(), calls=%async_computation | async-start | bytes 4456448 | tf_op jit(solution)/shard_map/all_gather | solution.py:56
  7.3 169.4 %all-reduce.2.cloned.1.call-start = ((), (), s32[]{:S(2)}) async-start(), calls=%async_computation.1 | async-start | bytes 8388608 | tf_op jit(solution)/shard_map/psum | solution.py:9
  64.8 0.7 copy-start.5
  64.8 0.7 copy-start.3
  64.8 0.8 copy-start.4
  64.8 0.9 copy-start.2
  65.7 8.2 %copy-start = (bf16[2,1024,1024]{2,1,0:T(8,128)(2,1)S(1)}, bf16[2,1024,1024]{2,1,0:T(8,128)(2,1)}, u32[]{:S(2)}) copy-start(bf16[2,1024,1024]{2,1,0:T(8,128)(2,1)} %all-gather.2.cloned.1.call-done) | copy-start | bytes 12582916
  179.9 1.6 copy-start.1
Sparse Core Ops, SparseCore 0:
  9.0 51.3 all-gather.1
  65.0 111.6 all-reduce.1
where the time goes:
time: 221 us
  waiting for transfers between devices  155 us (70%)
  matrix products  29 us (13%)
  other arithmetic  19.1 us (9%)
  between operations  13.5 us (6%)
  local copies, waits for them, and re-layouts  4.23 us (2%)
    psum x1, waiting for transfers between devices, broadcast(): return lax.psum(kept, axis)  101 us
    all_gather x1, waiting for transfers between devices, body(): lax.all_gather(pair_elements, ('row', 'freq'), axis=1, tiled=True)  53 us
    dot_general x2, matrix products, contribute(): lax.dot_general(imag_left, right_both, dims, preferred_element_type=jnp.f...  11.4 us
    another operation x3, other arithmetic, contribute(): return jnp.stack(results, 0)  11.3 us
    dot_general x2, matrix products, contribute(): lax.dot_general(real_left, right_both, dims, preferred_element_type=jnp.f...  9.55 us
    dot_general x4, matrix products, lookup(): return jnp.dot(onehot, flat, precision=lax.Precision.HIGHEST)  8.03 us
    select_n x1, other arithmetic, broadcast(): jnp.where(lax.axis_index(axis) == source, value, 0).astype(value.dtype)  4.47 us
  transfers between devices with their start and end apart: 2, of which 2 were waited for; matrix products, arithmetic and copies ran while one was open for 5% of the time, Pallas kernels for 0%

commit v1 on v0

v1 whole, which is shorter than its diff:
```python
import functools

import jax
import jax.numpy as jnp
from jax import lax
from jax.experimental import pallas as pl
from jax.experimental.pallas import tpu as pltpu
from jax.sharding import PartitionSpec as P

MESH = pl.DeviceIdType.MESH
SHIFT = (0, 1, 3, 2)
A1, A2, A3, A4, B1, B2, B3, B4 = range(0, 16, 2)


def where_am_i():
    row, col, low = lax.axis_index("row"), lax.axis_index("col"), lax.axis_index("freq")
    return col % 4, 2 * (col // 4) + low, row // 2, row % 2


def device(x, y, z, core):
    return (2 * (z % 4) + core, 4 * ((y % 4) // 2) + x % 4, y % 2)


def slot_of(y, z):
    delta = (y + 8 - 2 * (z // 2)) % 4
    return 2 * (delta // 2) + (delta + delta // 2) % 2


def gather_kernel(pair, rowp, colp, own_sem, s_send, s_recv, r_send, r_recv, c_send, c_recv, b_send, b_recv):
    x, y, z, core = where_am_i()
    low = y % 2
    half = pair.shape[2] // 2
    diagonal = (2 * z + core == 4 * (y // 2) + x) & (core == 0)
    target_z, target_core = 2 * (y // 2) + x // 2, x % 2
    target_y = (y + 4 + core * (2 * low - 1)) % 4
    mine = 2 * core + low
    partner = 2 * core + 1 - low
    xm, xp = (x + 3) % 4, (x + 1) % 4
    s0, sm, sp = slot_of(y, z), slot_of(y + 3, z), slot_of(y + 1, z)
    to_xp, to_xm = device(x + 1, y, z, core), device(x + 3, y, z, core)
    to_yp, to_ym = device(x, y + 1, z, core), device(x, y + 3, z, core)
    to_zp, to_zm = device(x, y, z + 1, core), device(x, y, z + 3, core)
    to_sibling = device(x, y, z, 1 - core)
    to_partner = device(x, y + 1 - 2 * low + 4, z, core)

    delta = (y + 8 - 2 * (z // 2)) % 4
    from_core, from_low = delta // 2, (delta + delta // 2) % 2
    from_x, from_y = 2 * (z % 2) + core, 2 * (z // 2) + from_low

    barrier = pltpu.get_barrier_semaphore()
    for there in (to_xp, to_xm, to_yp, to_ym, to_zp, to_zm, to_sibling):
        pl.semaphore_signal(barrier, inc=1, device_id=there, device_id_type=MESH)
    for q in range(4):
        @pl.when(jnp.logical_not(diagonal & (x == q)))
        def _():
            pl.semaphore_signal(
                barrier, inc=1, device_id=device(q, target_y, target_z, target_core), device_id_type=MESH
            )

        @pl.when(jnp.logical_not(diagonal & (z == q)))
        def _():
            pl.semaphore_signal(
                barrier, inc=1, device_id=device(from_x, from_y, q, from_core), device_id_type=MESH
            )
    pl.semaphore_wait(barrier, 15 - 2 * diagonal.astype(jnp.int32))

    sent = []

    def send(src, dst, sems, slot, there):
        copy = pltpu.make_async_remote_copy(
            src_ref=src, dst_ref=dst, send_sem=sems[0].at[slot], recv_sem=sems[1].at[slot],
            device_id=there, device_id_type=MESH,
        )
        copy.start()
        sent.append(copy)
        return copy

    rows, cols, both = (r_send, r_recv), (c_send, c_recv), (b_send, b_recv)

    def sibling(round_, slot, index):
        ref = colp.at[round_, :, slot]
        return send(ref, ref, both, index, to_sibling)

    own = pltpu.make_async_copy(pair, colp.at[0, :, mine], own_sem)
    own.start()
    c_part = send(pair, colp.at[0, :, mine], cols, 0, to_partner)
    shift = (z + 4 - target_z) % 4
    target_round = shift + (shift == 2).astype(jnp.int32) - (shift == 3).astype(jnp.int32)
    scatter = []
    for q in range(4):
        src = pair.at[:, pl.ds(16 * q, 16), :]
        dst = rowp.at[target_round, :, mine, q]
        remote = pltpu.make_async_remote_copy(
            src_ref=src, dst_ref=dst, send_sem=s_send.at[q], recv_sem=s_recv.at[target_round],
            device_id=device(q, target_y, target_z, target_core), device_id_type=MESH,
        )
        local = pltpu.make_async_copy(src, dst, s_recv.at[target_round])
        here = diagonal & (x == q)

        @pl.when(here)
        def _():
            local.start()

        @pl.when(jnp.logical_not(here))
        def _():
            remote.start()

        scatter.append((here, remote))
    c_zp = send(pair, colp.at[2, :, mine], cols, 1, to_zp)
    c_zm = send(pair, colp.at[1, :, mine], cols, 2, to_zm)
    s_own = send(pair, colp.at[0, :, mine], both, 0, to_sibling)
    waits = [s_own]

    gather = {}

    def step(stage, j):
        def ref(part, *index):
            return rowp.at[(j, part) + index]

        def go(name, ref, there):
            gather[j, name] = send(ref, ref, rows, 16 * j + name, there)

        def arrived(*names):
            for name in names:
                gather[j, name].wait_recv()
                gather[j, name + 1].wait_recv()

        if stage == 0:
            mine_ref = rowp.at[j, :, s0, x]
            pltpu.make_async_copy(mine_ref, mine_ref, s_recv.at[j]).wait()
            go(A1, ref(0, s0, x), to_xp)
            go(A1 + 1, ref(0, s0, x), to_xm)
            go(B1, ref(1, s0, x), to_yp)
            go(B1 + 1, ref(1, s0, x), to_ym)
        if stage == 1:
            first, second = pl.ds(0, half), pl.ds(half, half)
            arrived(A1)
            go(A2, ref(0, s0, xm, slice(None), first), to_xp)
            go(A2 + 1, ref(0, s0, xp, slice(None), second), to_xm)
            arrived(B1)
            go(B2, ref(1, sm, x, slice(None), first), to_yp)
            go(B2 + 1, ref(1, sp, x, slice(None), second), to_ym)
        if stage == 2:
            arrived(A2)
            go(A3, ref(0, s0), to_yp)
            go(A3 + 1, ref(0, s0), to_ym)
            arrived(B2)
            go(B3, ref(1, slice(None), x), to_xp)
            go(B3 + 1, ref(1, slice(None), x), to_xm)
        if stage == 3:
            arrived(A3)
            go(A4, ref(0, sm, pl.ds(0, 2)), to_yp)
            go(A4 + 1, ref(0, sp, pl.ds(2, 2)), to_ym)
            arrived(B3)
            go(B4, ref(1, pl.ds(0, 2), xm), to_xp)
            go(B4 + 1, ref(1, pl.ds(2, 2), xp), to_xm)
        if stage == 4:
            arrived(A4, B4)

    step(0, 0)
    step(0, 1)
    step(1, 0)
    step(0, 2)
    step(1, 1)
    step(2, 0)
    c_part.wait_recv()
    ref = colp.at[0, :, partner]
    c_zp2 = send(ref, colp.at[2, :, partner], cols, 3, to_zp)
    c_zm2 = send(ref, colp.at[1, :, partner], cols, 4, to_zm)
    waits.append(sibling(0, partner, 1))
    step(0, 3)
    step(1, 2)
    step(2, 1)
    step(3, 0)
    c_zp.wait_recv()
    c_far = send(colp.at[2, :, mine], colp.at[3, :, mine], cols, 5, to_zp)
    waits.append(sibling(2, mine, 2))
    c_zm.wait_recv()
    waits.append(sibling(1, mine, 3))
    step(1, 3)
    step(2, 2)
    step(3, 1)
    step(4, 0)
    c_zm2.wait_recv()
    c_far2 = send(colp.at[1, :, partner], colp.at[3, :, partner], cols, 6, to_zm)
    waits.append(sibling(1, partner, 4))
    c_zp2.wait_recv()
    waits.append(sibling(2, partner, 5))
    step(2, 3)
    step(3, 2)
    step(4, 1)
    c_far.wait_recv()
    waits.append(sibling(3, mine, 6))
    c_far2.wait_recv()
    waits.append(sibling(3, partner, 7))
    step(3, 3)
    step(4, 2)
    step(4, 3)
    for copy in waits:
        copy.wait_recv()
    own.wait()
    for copy in sent:
        copy.wait_send()
    for here, remote in scatter:
        @pl.when(jnp.logical_not(here))
        def _():
            remote.wait_send()


def find_weights(transitions, energies, occupations, frequencies, weight):
    count = transitions.shape[1]
    bands, points = energies.shape
    kpoint, valence, conduction = transitions[0:1, :], transitions[1:2, :], transitions[2:3, :]
    pick = (lax.broadcasted_iota(jnp.int32, (points, count), 0) == kpoint).astype(jnp.float32)
    band = lax.broadcasted_iota(jnp.int32, (bands, count), 0)

    def of(table):
        values = jnp.dot(table, pick, precision=lax.Precision.HIGHEST, preferred_element_type=jnp.float32)

        def one(which):
            return jnp.sum(jnp.where(band == which, values, 0.0), axis=0, keepdims=True)

        return one(valence), one(conduction)

    low, high = of(energies[...])
    gap = high - low
    below, above = of(occupations[...].astype(jnp.float32))
    filled = below - above
    for f in range(weight.shape[0]):
        frequency = frequencies[f]
        weight[f : f + 1, :] = filled * 2.0 * gap / (gap * gap + frequency * frequency)


def compute_kernel(rowp, colp, transitions, energies, occupations, frequencies, out, weight):
    z = where_am_i()[2]

    @pl.when(pl.program_id(0) == 0)
    def _():
        find_weights(transitions, energies, occupations, frequencies, weight)

    block = rowp.shape[-1]
    right = colp[...].reshape(-1, colp.shape[-1])
    lefts = [
        rowp[j, part].reshape(-1, block).T.astype(jnp.float32) for j in range(4) for part in range(2)
    ]
    for f in range(out.shape[0]):
        real, imag = [], []
        for j in range(4):
            depth = lefts[0].shape[1]
            start = pl.multiple_of(((z + SHIFT[j]) % 4) * depth, depth)
            w = weight[f : f + 1, pl.ds(start, depth)]
            first = (lefts[2 * j] * w).astype(jnp.bfloat16)
            second = (lefts[2 * j + 1] * w).astype(jnp.bfloat16)
            real += [first, second]
            imag += [second, -first]
        for part, pieces in enumerate((real, imag)):
            out[f, part] = jnp.dot(
                jnp.concatenate(pieces, axis=1), right, preferred_element_type=jnp.float32
            )


def body(pair_elements, transitions, energies, occupations, frequencies):
    width = pair_elements.shape[2]
    dma = pltpu.SemaphoreType.DMA
    rowp, colp = pl.pallas_call(
        gather_kernel,
        out_shape=(
            jax.ShapeDtypeStruct((4, 2, 4, 4, 16, width), jnp.bfloat16),
            jax.ShapeDtypeStruct((4, 2, 4, 64, width), jnp.bfloat16),
        ),
        in_specs=[pl.BlockSpec(memory_space=pltpu.VMEM)],
        out_specs=[pl.BlockSpec(memory_space=pltpu.VMEM)] * 2,
        scratch_shapes=[
            dma, dma((4,)), dma((4,)), dma((64,)), dma((64,)), dma((7,)), dma((7,)), dma((8,)), dma((8,)),
        ],
        compiler_params=pltpu.CompilerParams(collective_id=0, has_side_effects=True),
    )(pair_elements)
    block = 256
    count = transitions.shape[1]
    return pl.pallas_call(
        compute_kernel,
        grid=(width // block,),
        out_shape=jax.ShapeDtypeStruct((2, 2, width, width), jnp.float32),
        in_specs=[
            pl.BlockSpec((4, 2, 4, 4, 16, block), lambda i: (0, 0, 0, 0, 0, i)),
            pl.BlockSpec((4, 2, 4, 64, width), lambda i: (0, 0, 0, 0, 0), pipeline_mode=pl.Buffered(1)),
            pl.BlockSpec((3, count), lambda i: (0, 0)),
            pl.BlockSpec((64, 16), lambda i: (0, 0)),
            pl.BlockSpec((64, 16), lambda i: (0, 0)),
            pl.BlockSpec(memory_space=pltpu.SMEM),
        ],
        out_specs=pl.BlockSpec((2, 2, block, width), lambda i: (0, 0, i, 0)),
        scratch_shapes=[pltpu.VMEM((2, count), jnp.float32)],
        compiler_params=pltpu.CompilerParams(vmem_limit_bytes=48 * 2**20),
    )(rowp, colp, transitions, energies.T, occupations.T, frequencies)


def solution(mesh):
    in_specs = (P(None, ("row", "freq"), "col"), P(), P(), P(), P("freq"))
    out_specs = P("freq", None, "row", "col")
    return jax.shard_map(body, mesh=mesh, in_specs=in_specs, out_specs=out_specs, check_vma=False)
```

time: 221 us -> 75.8 us (0.34)
  waiting for transfers between devices: 155 us -> 0 us
  Pallas kernels: 0 us -> 70.3 us
  matrix products: 29 us -> 0 us
  other arithmetic: 19.1 us -> 0 us
  between operations: 13.5 us -> 0.02 us
    psum x1 -> x0, waiting for transfers between devices: 101 us -> none  [broadcast(): return lax.psum(kept, axis)]
    pallas_call x0 -> x2, Pallas kernels: none -> 70.3 us  [the longest x1 46.6 us: body(): pl.pallas_call(gather_kernel, out_shape=(jax.ShapeDtypeStruct((4, 2, 4, 4...]
    all_gather x1 -> x0, waiting for transfers between devices: 53 us -> none  [body(): lax.all_gather(pair_elements, ('row', 'freq'), axis=1, tiled=True)]
    dot_general x8 -> x0, matrix products: 29 us -> none  [the longest x2 11.4 us: contribute(): lax.dot_general(imag_left, right_both, dims, preferred_element_type=jnp.f...]
    another operation x3 -> x0, other arithmetic: 11.3 us -> none  [contribute(): return jnp.stack(results, 0)]
    select_n x1 -> x0, other arithmetic: 4.47 us -> none  [broadcast(): jnp.where(lax.axis_index(axis) == source, value, 0).astype(value.dtype)]
    unnamed x12 -> x8, local copies, waits for them, and re-layouts: 1.13 us -> 5.11 us
    convert_element_type x2 -> x0, other arithmetic: 2.95 us -> none  [the longest x1 2.95 us: contribute(): (left.astype(jnp.float32) * weight_block[index][None, :, None]).astype(jn...]
  transfers between devices with their start and end apart: 2 -> 0, of which waited for: 2 -> 0; matrix products, arithmetic and copies ran while one was open for 5% -> 0% of each run, Pallas kernels for 0% -> 0%
where the time goes in v1:
time: 75.8 us; the launch traced here: 75.4 us
  Pallas kernels  70.3 us (93%)
  local copies, waits for them, and re-layouts  5.11 us (7%)
    pallas_call x1, Pallas kernels, body(): pl.pallas_call(gather_kernel, out_shape=(jax.ShapeDtypeStruct((4, 2, 4, 4...  46.6 us
    pallas_call x1, Pallas kernels, body(): pl.pallas_call(compute_kernel, grid=(width // block,), out_shape=jax.Shap...  23.7 us
    unnamed x8, local copies, waits for them, and re-layouts  5.11 us

profile of v1, /device:TPU:0, one launch (start us, length us, event | category | flops | bytes accessed | tf_op | source)
XLA Modules:
  0.0 75.4 jit_solution(2670346505136032021)
XLA Ops:
  0.0 0.8 %copy.6 = f32[16,64]{0,1:T(8,128)S(1)} copy(f32[16,64]{1,0:T(8,128)} %param.7) | data formatting | bytes 8192 | tf_op args[2]
  0.8 0.8 %copy.7 = s32[16,64]{0,1:T(8,128)S(1)} copy(s32[16,64]{1,0:T(8,128)} %param.8) | data formatting | bytes 8192 | tf_op args[3]
  1.6 46.6 %shard_map.55 = (bf16[4,2,4,4,16,1024]{5,4,3,2,1,0:T(8,128)(2,1)}, bf16[4,2,4,64,1024]{4,3,2,1,0:T(8,128)(2,1)}) custom-call(bf16[2,64,1024]{2,1,0:T(8,128)(2,1)} %pair.1), custom_call_target="tpu_custom_call" | custom-call | tf_op jit(solution)/shard_map/pallas_call | solution.py:265
  48.2 0.0 copy-start
  48.2 2.2 %copy-done = bf16[4,2,4,4,16,1024]{5,4,3,2,1,0:T(8,128)(2,1)S(1)} copy-done((bf16[4,2,4,4,16,1024]{5,4,3,2,1,0:T(8,128)(2,1)S(1)}, bf16[4,2,4,4,16,1024]{5,4,3,2,1,0:T(8,128)(2,1)}, u32[]{:S(2)}) %copy-start) | copy-done | bytes 4194328
  50.4 0.0 copy-start.1
  50.4 0.7 copy-done.1
  51.1 0.0 copy-start.2
  51.1 0.7 copy-done.2
  51.7 23.7 %shard_map.56 = f32[2,2,1024,1024]{3,2,1,0:T(8,128)} custom-call(bf16[4,2,4,4,16,1024]{5,4,3,2,1,0:T(8,128)(2,1)S(1)} %copy-done, bf16[4,2,4,64,1024]{4,3,2,1,0:T(8,128)(2,1)} %get-tuple-element.8.colp, s32[3,1024]{1,0:T(4,128)S(1)} %copy-done.1, f32[64,16]{1,0:T(8,128)S(1)} %bitcast.2, s32[64,16]{1,0:T(8,128)S(1)} %bitcast.3, f32[2]{0:T(128)S(1)} %copy-done.2), custom_call_target="tpu_custom_call" | custom-call | tf_op jit(solution)/shard_map/pallas_call | solution.py:280
Async XLA Ops:
  48.2 2.2 %copy-start = (bf16[4,2,4,4,16,1024]{5,4,3,2,1,0:T(8,128)(2,1)S(1)}, bf16[4,2,4,4,16,1024]{5,4,3,2,1,0:T(8,128)(2,1)}, u32[]{:S(2)}) copy-start(bf16[4,2,4,4,16,1024]{5,4,3,2,1,0:T(8,128)(2,1)} %get-tuple-element.7.rowp) | copy-start | bytes 12582916
  50.4 0.7 copy-start.1
  51.1 0.7 copy-start.2

commit v2 on v1

v2 whole, which is shorter than its diff:
```python
import functools

import jax
import jax.numpy as jnp
from jax import lax
from jax.experimental import pallas as pl
from jax.experimental.pallas import tpu as pltpu
from jax.sharding import PartitionSpec as P

MESH = pl.DeviceIdType.MESH
ORDER = (
    (0, 0), (0, 1), (1, 0), (0, 2), (1, 1), (2, 0), ("c", 0), (0, 3), (1, 2), (2, 1), (3, 0), ("c", 1), (1, 3),
    (2, 2), (3, 1), (4, 0), ("c", 2), ("k", 0), (2, 3), (3, 2), ("k", 1), (4, 1), ("c", 3), ("k", 2), (3, 3), ("k", 3),
    (4, 2), ("k", 4), ("k", 5), (4, 3),
)

TILE = 256
SHIFT = (0, 1, 3, 2)
A1, A2, A3, A4, B1, B2, B3, B4 = range(0, 16, 2)


def where_am_i():
    row, col, low = lax.axis_index("row"), lax.axis_index("col"), lax.axis_index("freq")
    return col % 4, 2 * (col // 4) + low, row // 2, row % 2


def device(x, y, z, core):
    return (2 * (z % 4) + core, 4 * ((y % 4) // 2) + x % 4, y % 2)


def slot_of(y, z):
    delta = (y + 8 - 2 * (z // 2)) % 4
    return 2 * (delta // 2) + (delta + delta // 2) % 2


def gather_kernel(
    pair, transitions, energies, occupations, frequencies, rowp, colp, weight, total, own_sem, s_send, s_recv, r_send, r_recv, c_send, c_recv,
    b_send, b_recv,
):
    x, y, z, core = where_am_i()
    low = y % 2
    half = pair.shape[2] // 2
    diagonal = (2 * z + core == 4 * (y // 2) + x) & (core == 0)
    target_z, target_core = 2 * (y // 2) + x // 2, x % 2
    target_y = (y + 4 + core * (2 * low - 1)) % 4
    mine = 2 * core + low
    partner = 2 * core + 1 - low
    xm, xp = (x + 3) % 4, (x + 1) % 4
    y_pair, y_next = y + 1 - 2 * low, y + 3 + 2 * low
    s0, s_pair, s_next = slot_of(y, z), slot_of(y_pair, z), slot_of(y_next, z)
    to_partner, to_next = device(x, y_pair, z, core), device(x, y_next, z, core)
    to_xp, to_xm = device(x + 1, y, z, core), device(x + 3, y, z, core)
    to_zp, to_zm = device(x, y, z + 1, core), device(x, y, z + 3, core)
    to_sibling = device(x, y, z, 1 - core)

    delta = (y + 8 - 2 * (z // 2)) % 4
    from_core, from_low = delta // 2, (delta + delta // 2) % 2
    from_x, from_y = 2 * (z % 2) + core, 2 * (z // 2) + from_low

    barrier = pltpu.get_barrier_semaphore()
    for there in (to_xp, to_xm, to_partner, to_next, to_zp, to_zm, to_sibling):
        pl.semaphore_signal(barrier, inc=1, device_id=there, device_id_type=MESH)
    for q in range(4):
        @pl.when(jnp.logical_not(diagonal & (x == q)))
        def _():
            pl.semaphore_signal(
                barrier, inc=1, device_id=device(q, target_y, target_z, target_core), device_id_type=MESH
            )

        @pl.when(jnp.logical_not(diagonal & (z == q)))
        def _():
            pl.semaphore_signal(
                barrier, inc=1, device_id=device(from_x, from_y, q, from_core), device_id_type=MESH
            )
    find_weights(transitions, energies, occupations, frequencies, weight)
    pl.semaphore_wait(barrier, 15 - 2 * diagonal.astype(jnp.int32))

    sent = []

    def send(src, dst, sems, slot, there):
        copy = pltpu.make_async_remote_copy(
            src_ref=src, dst_ref=dst, send_sem=sems[0].at[slot], recv_sem=sems[1].at[slot],
            device_id=there, device_id_type=MESH,
        )
        copy.start()
        sent.append(copy)
        return copy

    rows, cols, both = (r_send, r_recv), (c_send, c_recv), (b_send, b_recv)

    def sibling(round_, slot, index):
        ref = colp.at[round_, :, slot]
        return send(ref, ref, both, index, to_sibling)

    own = pltpu.make_async_copy(pair, colp.at[0, :, mine], own_sem)
    own.start()
    c_part = send(pair, colp.at[0, :, mine], cols, 0, to_partner)
    shift = (z + 4 - target_z) % 4
    target_round = shift + (shift == 2).astype(jnp.int32) - (shift == 3).astype(jnp.int32)
    scatter = []
    for q in range(4):
        src = pair.at[:, pl.ds(16 * q, 16), :]
        dst = rowp.at[target_round, :, mine, q]
        remote = pltpu.make_async_remote_copy(
            src_ref=src, dst_ref=dst, send_sem=s_send.at[q], recv_sem=s_recv.at[target_round],
            device_id=device(q, target_y, target_z, target_core), device_id_type=MESH,
        )
        local = pltpu.make_async_copy(src, dst, s_recv.at[target_round])
        here = diagonal & (x == q)

        @pl.when(here)
        def _():
            local.start()

        @pl.when(jnp.logical_not(here))
        def _():
            remote.start()

        scatter.append((here, remote))
    c_zp = send(pair, colp.at[2, :, mine], cols, 1, to_zp)
    c_zm = send(pair, colp.at[1, :, mine], cols, 2, to_zm)
    s_own = send(pair, colp.at[0, :, mine], both, 0, to_sibling)
    waits = [s_own]
    needed = ((0, 1), (3, 4), (2, 5), (6, 7))

    gather = {}

    def step(stage, j):
        def ref(part, *index):
            return rowp.at[(j, part) + index]

        def go(name, ref, there):
            gather[j, name] = send(ref, ref, rows, 16 * j + name, there)

        def arrived(*names):
            for name in names:
                gather[j, name].wait_recv()
                gather[j, name + 1].wait_recv()

        if stage == 0:
            mine_ref = rowp.at[j, :, s0, x]
            pltpu.make_async_copy(mine_ref, mine_ref, s_recv.at[j]).wait()
            go(A1, ref(0, s0, x), to_xp)
            go(A1 + 1, ref(0, s0, x), to_xm)
            go(B1, ref(1, s0, x), to_partner)
            go(B1 + 1, ref(1, s0, x), to_next)
        if stage == 1:
            first, second = pl.ds(0, half), pl.ds(half, half)
            arrived(A1)
            go(A2, ref(0, s0, xm, slice(None), first), to_xp)
            go(A2 + 1, ref(0, s0, xp, slice(None), second), to_xm)
            arrived(B1)
            go(B2, ref(1, s_next, x, slice(None), first), to_partner)
            go(B2 + 1, ref(1, s_pair, x, slice(None), second), to_next)
        if stage == 2:
            arrived(A2)
            go(A3, ref(0, s0), to_partner)
            go(A3 + 1, ref(0, s0), to_next)
            arrived(B2)
            go(B3, ref(1, slice(None), x), to_xp)
            go(B3 + 1, ref(1, slice(None), x), to_xm)
        if stage == 3:
            arrived(A3)
            go(A4, ref(0, s_next, pl.ds(0, 1)), to_partner)
            go(A4 + 1, ref(0, s_pair, pl.ds(1, 3)), to_next)
            arrived(B3)
            go(B4, ref(1, pl.ds(0, 2), xm), to_xp)
            go(B4 + 1, ref(1, pl.ds(2, 2), xp), to_xm)
        if stage == 4:
            arrived(A4, B4)

    held = {}

    def col_event(n):
        if n == 0:
            c_part.wait_recv()
            ref = colp.at[0, :, partner]
            held["zp2"] = send(ref, colp.at[2, :, partner], cols, 3, to_zp)
            held["zm2"] = send(ref, colp.at[1, :, partner], cols, 4, to_zm)
            waits.append(sibling(0, partner, 1))
        if n == 1:
            c_zp.wait_recv()
            held["far"] = send(colp.at[2, :, mine], colp.at[3, :, mine], cols, 5, to_zp)
            waits.append(sibling(2, mine, 2))
            c_zm.wait_recv()
            waits.append(sibling(1, mine, 3))
        if n == 2:
            held["zm2"].wait_recv()
            held["far2"] = send(colp.at[1, :, partner], colp.at[3, :, partner], cols, 6, to_zm)
            waits.append(sibling(1, partner, 4))
            held["zp2"].wait_recv()
            waits.append(sibling(2, partner, 5))
        if n == 3:
            held["far"].wait_recv()
            waits.append(sibling(3, mine, 6))
            held["far2"].wait_recv()
            waits.append(sibling(3, partner, 7))

    for name, n in ORDER:
        if name == "c":
            col_event(n)
        elif name == "k":
            j = n // 2
            if n == 0:
                own.wait()
            if n % 2 == 0:
                for index in needed[j]:
                    waits[index].wait_recv()
            for tile in (n % 2 * 2, n % 2 * 2 + 1):
                for f, part, span, product in products(rowp, colp, weight, z, j, tile):
                    if j == 0:
                        total[f, part, span, :] = product
                    else:
                        total[f, part, span, :] += product
        else:
            step(name, n)
    for index in needed[3]:
        waits[index].wait_recv()
    for copy in sent:
        copy.wait_send()
    for here, remote in scatter:
        @pl.when(jnp.logical_not(here))
        def _():
            remote.wait_send()


def find_weights(transitions, energies, occupations, frequencies, weight):
    count = transitions.shape[1]
    bands, points = energies.shape
    kpoint, valence, conduction = transitions[0:1, :], transitions[1:2, :], transitions[2:3, :]
    pick = (lax.broadcasted_iota(jnp.int32, (points, count), 0) == kpoint).astype(jnp.float32)
    band = lax.broadcasted_iota(jnp.int32, (bands, count), 0)

    def of(table):
        values = jnp.dot(table, pick, precision=lax.Precision.HIGHEST, preferred_element_type=jnp.float32)

        def one(which):
            return jnp.sum(jnp.where(band == which, values, 0.0), axis=0, keepdims=True)

        return one(valence), one(conduction)

    low, high = of(energies[...])
    gap = high - low
    below, above = of(occupations[...].astype(jnp.float32))
    filled = below - above
    for f in range(weight.shape[0]):
        frequency = frequencies[f]
        weight[f : f + 1, :] = filled * 2.0 * gap / (gap * gap + frequency * frequency)


def products(rowp, colp, weight, z, j, tile):
    rows = pl.ds(TILE * tile, TILE)
    right = colp[j].reshape(-1, colp.shape[-1])
    depth = right.shape[0] // 2
    lefts = [rowp[j, part, :, :, :, rows].reshape(depth, TILE).T.astype(jnp.float32) for part in range(2)]
    start = pl.multiple_of(((z + SHIFT[j]) % 4) * depth, depth)
    for f in range(weight.shape[0]):
        w = weight[f : f + 1, pl.ds(start, depth)]
        first, second = [(left * w).astype(jnp.bfloat16) for left in lefts]
        for part, pair in enumerate(((first, second), (second, -first))):
            yield f, part, rows, jnp.dot(jnp.concatenate(pair, axis=1), right, preferred_element_type=jnp.float32)


def finish_kernel(rowp, colp, weight, total, out, stage, sems):
    z = where_am_i()[2]
    copies = []
    for tile in range(total.shape[2] // TILE):
        for f, part, rows, product in products(rowp, colp, weight, z, 3, tile):
            stage[f, part, rows, :] = total[f, part, rows, :] + product
            copy = pltpu.make_async_copy(
                stage.at[f, part, rows, :], out.at[f, part, rows, :], sems.at[tile, f, part]
            )
            copy.start()
            copies.append(copy)
    for copy in copies:
        copy.wait()


def body(pair_elements, transitions, energies, occupations, frequencies):
    width = pair_elements.shape[2]
    dma = pltpu.SemaphoreType.DMA
    vmem, smem = pl.BlockSpec(memory_space=pltpu.VMEM), pl.BlockSpec(memory_space=pltpu.SMEM)
    kept = pl.pallas_call(
        gather_kernel,
        out_shape=(
            pltpu.VMEM((4, 2, 4, 4, 16, width), jnp.bfloat16),
            pltpu.VMEM((4, 2, 4, 64, width), jnp.bfloat16),
            pltpu.VMEM((2, transitions.shape[1]), jnp.float32),
            pltpu.VMEM((2, 2, width, width), jnp.float32),
        ),
        in_specs=[vmem] * 4 + [smem],
        out_specs=[vmem] * 4,
        scratch_shapes=[
            dma, dma((4,)), dma((4,)), dma((64,)), dma((64,)), dma((7,)), dma((7,)), dma((8,)), dma((8,)),
        ],
        compiler_params=pltpu.CompilerParams(
            collective_id=0, has_side_effects=True, vmem_limit_bytes=8 * 2**20
        ),
    )(pair_elements, transitions, energies.T, occupations.T, frequencies)
    return pl.pallas_call(
        finish_kernel,
        out_shape=jax.ShapeDtypeStruct((2, 2, width, width), jnp.float32),
        in_specs=[vmem] * 4,
        out_specs=pl.BlockSpec(memory_space=pl.ANY),
        scratch_shapes=[pltpu.VMEM((2, 2, width, width), jnp.float32), dma((width // TILE, 2, 2))],
        compiler_params=pltpu.CompilerParams(vmem_limit_bytes=24 * 2**20),
    )(*kept)


def solution(mesh):
    in_specs = (P(None, ("row", "freq"), "col"), P(), P(), P(), P("freq"))
    out_specs = P("freq", None, "row", "col")
    return jax.shard_map(body, mesh=mesh, in_specs=in_specs, out_specs=out_specs, check_vma=False)
```

time: 75.8 us -> 58.8 us (0.78)
  Pallas kernels: 70.3 us -> 54.4 us
  local copies, waits for them, and re-layouts: 5.11 us -> 3.88 us
    pallas_call x2, Pallas kernels: 70.3 us -> 54.4 us  [the longest x1 47.9 us: body(): pl.pallas_call(gather_kernel, out_shape=(pltpu.VMEM((4, 2, 4, 4, 16, widt...]
    unnamed x8, local copies, waits for them, and re-layouts: 5.11 us -> 3.88 us
where the time goes in v2:
time: 58.8 us; the launch traced here: 58.4 us
  Pallas kernels  54.4 us (93%)
  local copies, waits for them, and re-layouts  3.88 us (7%)
    pallas_call x1, Pallas kernels, body(): pl.pallas_call(gather_kernel, out_shape=(pltpu.VMEM((4, 2, 4, 4, 16, widt...  47.9 us
    pallas_call x1, Pallas kernels, body(): pl.pallas_call(finish_kernel, out_shape=jax.ShapeDtypeStruct((2, 2, width...  6.46 us
    unnamed x8, local copies, waits for them, and re-layouts  3.88 us

profile of v2, /device:TPU:0, one launch (start us, length us, event | category | flops | bytes accessed | tf_op | source)
XLA Modules:
  0.0 58.4 jit_solution(17558840660033627142)
XLA Ops:
  0.0 0.8 %copy.6 = f32[16,64]{0,1:T(8,128)S(1)} copy(f32[16,64]{1,0:T(8,128)} %param.7) | data formatting | bytes 8192 | tf_op args[2]
  0.8 0.8 %copy.7 = s32[16,64]{0,1:T(8,128)S(1)} copy(s32[16,64]{1,0:T(8,128)} %param.8) | data formatting | bytes 8192 | tf_op args[3]
  1.6 0.0 copy-start
  1.6 0.9 %copy-done = bf16[2,64,1024]{2,1,0:T(8,128)(2,1)S(1)} copy-done((bf16[2,64,1024]{2,1,0:T(8,128)(2,1)S(1)}, bf16[2,64,1024]{2,1,0:T(8,128)(2,1)}, u32[]{:S(2)}) %copy-start) | copy-done | bytes 262168
  2.5 0.0 copy-start.1
  2.5 0.7 %copy-done.1 = s32[3,1024]{1,0:T(4,128)S(1)} copy-done((s32[3,1024]{1,0:T(4,128)S(1)}, s32[3,1024]{1,0:T(4,128)}, u32[]{:S(2)}) %copy-start.1) | copy-done | bytes 12312
  3.2 0.0 copy-start.2
  3.2 0.7 %copy-done.2 = f32[2]{0:T(128)S(1)} copy-done((f32[2]{0:T(128)S(1)}, f32[2]{0:T(128)}, u32[]{:S(2)}) %copy-start.2) | copy-done | bytes 32
  3.9 47.9 %shard_map.55 = (bf16[4,2,4,4,16,1024]{5,4,3,2,1,0:T(8,128)(2,1)S(1)}, bf16[4,2,4,64,1024]{4,3,2,1,0:T(8,128)(2,1)S(1)}, f32[2,1024]{1,0:T(2,128)S(1)}, f32[2,2,1024,1024]{3,2,1,0:T(8,128)S(1)}) custom-call(bf16[2,64,1024]{2,1,0:T(8,128)(2,1)S(1)} %copy-done, s32[3,1024]{1,0:T(4,128)S(1)} %copy-done.1, f32[64,16]{1,0:T(8,128)S(1)} %bitcast.2, ...), custom_call_target="tpu_custom_call" | custom-call | tf_op jit(solution)/shard_map/pallas_call | solution.py:283
  51.8 6.5 %shard_map.56 = f32[2,2,1024,1024]{3,2,1,0:T(8,128)} custom-call(bf16[4,2,4,4,16,1024]{5,4,3,2,1,0:T(8,128)(2,1)S(1)} %get-tuple-element.9.rowp, bf16[4,2,4,64,1024]{4,3,2,1,0:T(8,128)(2,1)S(1)} %get-tuple-element.10.colp, f32[2,1024]{1,0:T(2,128)S(1)} %get-tuple-element.11.weight, f32[2,2,1024,1024]{3,2,1,0:T(8,128)S(1)} %get-tuple-element.12.total), custom_call_target="tpu_custom_call" | custom-call | tf_op jit(solution)/shard_map/pallas_call | solution.py:300
Async XLA Ops:
  1.6 1.0 %copy-start = (bf16[2,64,1024]{2,1,0:T(8,128)(2,1)S(1)}, bf16[2,64,1024]{2,1,0:T(8,128)(2,1)}, u32[]{:S(2)}) copy-start(bf16[2,64,1024]{2,1,0:T(8,128)(2,1)} %pair.1) | copy-start | bytes 786436
  2.5 0.7 %copy-start.1 = (s32[3,1024]{1,0:T(4,128)S(1)}, s32[3,1024]{1,0:T(4,128)}, u32[]{:S(2)}) copy-start(s32[3,1024]{1,0:T(4,128)} %transitions.1) | copy-start | bytes 36868
  3.2 0.7 %copy-start.2 = (f32[2]{0:T(128)S(1)}, f32[2]{0:T(128)}, u32[]{:S(2)}) copy-start(f32[2]{0:T(128)} %frequencies.1) | copy-start | bytes 28

commit v3 on v2

--- a/solution.py
+++ b/solution.py
@@ -1,5 +1,3 @@
-import functools
-
 import jax
 import jax.numpy as jnp
 from jax import lax
@@ -9,9 +7,9 @@
 
 MESH = pl.DeviceIdType.MESH
 ORDER = (
-    (0, 0), (0, 1), (1, 0), (0, 2), (1, 1), (2, 0), ("c", 0), (0, 3), (1, 2), (2, 1), (3, 0), ("c", 1), (1, 3),
-    (2, 2), (3, 1), (4, 0), ("c", 2), ("k", 0), (2, 3), (3, 2), ("k", 1), (4, 1), ("c", 3), ("k", 2), (3, 3), ("k", 3),
-    (4, 2), ("k", 4), ("k", 5), (4, 3),
+    "p0", "z0", "a00", "b00", "p1", "a01", "b01", "a10", "b10", "a02", "b02", "a11", "b11", "a20", "b20", "q0", "q1",
+    "a03", "b03", "a12", "b12", "a21", "b21", "a30", "b30", "c1", "a13", "b13", "a22", "b22", "e0", "a31", "b31",
+    "c2", "k0", "a23", "b23", "a32", "b32", "e1", "k1", "a33", "b33", "e2", "c3", "k2", "e3",
 )
 
 TILE = 256
@@ -34,10 +32,20 @@
 
 
 def gather_kernel(
-    pair, transitions, energies, occupations, frequencies, rowp, colp, weight, total, own_sem, s_send, s_recv, r_send, r_recv, c_send, c_recv,
-    b_send, b_recv,
+    pair_hbm, transitions_hbm, energies_hbm, occupations_hbm, frequencies_hbm, rowp, colp, weight, total,
+    pair, transitions, energies, occupations, frequencies, in_sem, own_sem, s_send, s_recv, r_send, r_recv,
+    c_send, c_recv, b_send, b_recv,
 ):
     x, y, z, core = where_am_i()
+    loads = [
+        pltpu.make_async_copy(src, dst, in_sem.at[i])
+        for i, (src, dst) in enumerate((
+            (pair_hbm, pair), (transitions_hbm, transitions), (energies_hbm, energies),
+            (occupations_hbm, occupations), (frequencies_hbm, frequencies),
+        ))
+    ]
+    for load in loads:
+        load.start()
     low = y % 2
     half = pair.shape[2] // 2
     diagonal = (2 * z + core == 4 * (y // 2) + x) & (core == 0)
@@ -72,6 +80,8 @@
             pl.semaphore_signal(
                 barrier, inc=1, device_id=device(from_x, from_y, q, from_core), device_id_type=MESH
             )
+    for load in loads:
+        load.wait()
     find_weights(transitions, energies, occupations, frequencies, weight)
     pl.semaphore_wait(barrier, 15 - 2 * diagonal.astype(jnp.int32))
 
@@ -94,7 +104,6 @@
 
     own = pltpu.make_async_copy(pair, colp.at[0, :, mine], own_sem)
     own.start()
-    c_part = send(pair, colp.at[0, :, mine], cols, 0, to_partner)
     shift = (z + 4 - target_z) % 4
     target_round = shift + (shift == 2).astype(jnp.int32) - (shift == 3).astype(jnp.int32)
     scatter = []
@@ -117,11 +126,9 @@
             remote.start()
 
         scatter.append((here, remote))
-    c_zp = send(pair, colp.at[2, :, mine], cols, 1, to_zp)
-    c_zm = send(pair, colp.at[1, :, mine], cols, 2, to_zm)
-    s_own = send(pair, colp.at[0, :, mine], both, 0, to_sibling)
-    waits = [s_own]
     needed = ((0, 1), (3, 4), (2, 5), (6, 7))
+    waits = {}
+    held = {}
 
     gather = {}
 
@@ -137,78 +144,94 @@
                 gather[j, name].wait_recv()
                 gather[j, name + 1].wait_recv()
 
-        if stage == 0:
+        first, second = pl.ds(0, half), pl.ds(half, half)
+        if stage in ("a0", "b0") and ("s", j) not in held:
+            held["s", j] = True
             mine_ref = rowp.at[j, :, s0, x]
             pltpu.make_async_copy(mine_ref, mine_ref, s_recv.at[j]).wait()
+        if stage == "a0":
             go(A1, ref(0, s0, x), to_xp)
             go(A1 + 1, ref(0, s0, x), to_xm)
+        if stage == "b0":
             go(B1, ref(1, s0, x), to_partner)
             go(B1 + 1, ref(1, s0, x), to_next)
-        if stage == 1:
-            first, second = pl.ds(0, half), pl.ds(half, half)
-            arrived(A1)
+        if stage == "a1":
+            gather[j, A1].wait_recv()
             go(A2, ref(0, s0, xm, slice(None), first), to_xp)
+            gather[j, A1 + 1].wait_recv()
             go(A2 + 1, ref(0, s0, xp, slice(None), second), to_xm)
-            arrived(B1)
+        if stage == "b1":
+            gather[j, B1 + 1].wait_recv()
             go(B2, ref(1, s_next, x, slice(None), first), to_partner)
+            gather[j, B1].wait_recv()
             go(B2 + 1, ref(1, s_pair, x, slice(None), second), to_next)
-        if stage == 2:
+        if stage == "a2":
             arrived(A2)
             go(A3, ref(0, s0), to_partner)
             go(A3 + 1, ref(0, s0), to_next)
+        if stage == "b2":
             arrived(B2)
             go(B3, ref(1, slice(None), x), to_xp)
             go(B3 + 1, ref(1, slice(None), x), to_xm)
-        if stage == 3:
-            arrived(A3)
+        if stage == "a3":
+            gather[j, A3].wait_recv()
+            go(A4 + 1, ref(0, s_pair, pl.ds(1, 3)), to_next)
+            gather[j, A3 + 1].wait_recv()
             go(A4, ref(0, s_next, pl.ds(0, 1)), to_partner)
-            go(A4 + 1, ref(0, s_pair, pl.ds(1, 3)), to_next)
-            arrived(B3)
+        if stage == "b3":
+            gather[j, B3].wait_recv()
             go(B4, ref(1, pl.ds(0, 2), xm), to_xp)
+            gather[j, B3 + 1].wait_recv()
             go(B4 + 1, ref(1, pl.ds(2, 2), xp), to_xm)
-        if stage == 4:
+        if stage == "e":
             arrived(A4, B4)
 
-    held = {}
-
-    def col_event(n):
-        if n == 0:
-            c_part.wait_recv()
-            ref = colp.at[0, :, partner]
-            held["zp2"] = send(ref, colp.at[2, :, partner], cols, 3, to_zp)
-            held["zm2"] = send(ref, colp.at[1, :, partner], cols, 4, to_zm)
-            waits.append(sibling(0, partner, 1))
-        if n == 1:
-            c_zp.wait_recv()
-            held["far"] = send(colp.at[2, :, mine], colp.at[3, :, mine], cols, 5, to_zp)
-            waits.append(sibling(2, mine, 2))
-            c_zm.wait_recv()
-            waits.append(sibling(1, mine, 3))
-        if n == 2:
-            held["zm2"].wait_recv()
-            held["far2"] = send(colp.at[1, :, partner], colp.at[3, :, partner], cols, 6, to_zm)
-            waits.append(sibling(1, partner, 4))
-            held["zp2"].wait_recv()
-            waits.append(sibling(2, partner, 5))
-        if n == 3:
+    def col_event(name, n):
+        if name == "p":
+            held["p", n] = send(pair.at[n], colp.at[0, n, mine], cols, n, to_partner)
+        if name == "z":
+            held["zp"] = send(pair, colp.at[2, :, mine], cols, 2, to_zp)
+            held["zm"] = send(pair, colp.at[1, :, mine], cols, 3, to_zm)
+            waits[0] = send(pair, colp.at[0, :, mine], both, 0, to_sibling)
+        if name == "q":
+            held["p", n].wait_recv()
+            ref = colp.at[0, n, partner]
+            held["zp", n] = send(ref, colp.at[2, n, partner], cols, 4 + n, to_zp)
+            held["zm", n] = send(ref, colp.at[1, n, partner], cols, 6 + n, to_zm)
+            if n == 1:
+                waits[1] = sibling(0, partner, 1)
+        if name == "c" and n == 1:
+            held["zp"].wait_recv()
+            held["far"] = send(colp.at[2, :, mine], colp.at[3, :, mine], cols, 8, to_zp)
+            waits[2] = sibling(2, mine, 2)
+            held["zm"].wait_recv()
+            waits[3] = sibling(1, mine, 3)
+        if name == "c" and n == 2:
+            for h in range(2):
+                held["zm", h].wait_recv()
+            held["far2"] = send(colp.at[1, :, partner], colp.at[3, :, partner], cols, 9, to_zm)
+            waits[4] = sibling(1, partner, 4)
+            for h in range(2):
+                held["zp", h].wait_recv()
+            waits[5] = sibling(2, partner, 5)
+        if name == "c" and n == 3:
             held["far"].wait_recv()
-            waits.append(sibling(3, mine, 6))
+            waits[6] = sibling(3, mine, 6)
             held["far2"].wait_recv()
-            waits.append(sibling(3, partner, 7))
-
-    for name, n in ORDER:
-        if name == "c":
-            col_event(n)
+            waits[7] = sibling(3, partner, 7)
+
+    for word in ORDER:
+        name, n = word[:-1], int(word[-1])
+        if name in "pzqc":
+            col_event(name, n)
         elif name == "k":
-            j = n // 2
             if n == 0:
                 own.wait()
-            if n % 2 == 0:
-                for index in needed[j]:
-                    waits[index].wait_recv()
-            for tile in (n % 2 * 2, n % 2 * 2 + 1):
-                for f, part, span, product in products(rowp, colp, weight, z, j, tile):
-                    if j == 0:
+            for index in needed[n]:
+                waits[index].wait_recv()
+            for tile in range(total.shape[2] // TILE):
+                for f, part, span, product in products(rowp, colp, weight, z, n, tile):
+                    if n == 0:
                         total[f, part, span, :] = product
                     else:
                         total[f, part, span, :] += product
@@ -226,13 +249,15 @@
 
 def find_weights(transitions, energies, occupations, frequencies, weight):
     count = transitions.shape[1]
-    bands, points = energies.shape
+    points, bands = energies.shape
     kpoint, valence, conduction = transitions[0:1, :], transitions[1:2, :], transitions[2:3, :]
     pick = (lax.broadcasted_iota(jnp.int32, (points, count), 0) == kpoint).astype(jnp.float32)
     band = lax.broadcasted_iota(jnp.int32, (bands, count), 0)
 
     def of(table):
-        values = jnp.dot(table, pick, precision=lax.Precision.HIGHEST, preferred_element_type=jnp.float32)
+        values = lax.dot_general(
+            table, pick, (((0,), (0,)), ((), ())), precision=lax.Precision.HIGHEST, preferred_element_type=jnp.float32
+        )
 
         def one(which):
             return jnp.sum(jnp.where(band == which, values, 0.0), axis=0, keepdims=True)
@@ -279,7 +304,11 @@
 def body(pair_elements, transitions, energies, occupations, frequencies):
     width = pair_elements.shape[2]
     dma = pltpu.SemaphoreType.DMA
-    vmem, smem = pl.BlockSpec(memory_space=pltpu.VMEM), pl.BlockSpec(memory_space=pltpu.SMEM)
+    vmem = pl.BlockSpec(memory_space=pltpu.VMEM)
+    inputs = [
+        pltpu.with_memory_space_constraint(value, pltpu.HBM)
+        for value in (pair_elements, transitions, energies, occupations, frequencies)
+    ]
     kept = pl.pallas_call(
         gather_kernel,
         out_shape=(
@@ -288,15 +317,20 @@
             pltpu.VMEM((2, transitions.shape[1]), jnp.float32),
             pltpu.VMEM((2, 2, width, width), jnp.float32),
         ),
-        in_specs=[vmem] * 4 + [smem],
+        in_specs=[pl.BlockSpec(memory_space=pltpu.HBM)] * 5,
         out_specs=[vmem] * 4,
         scratch_shapes=[
-            dma, dma((4,)), dma((4,)), dma((64,)), dma((64,)), dma((7,)), dma((7,)), dma((8,)), dma((8,)),
+            pltpu.VMEM(pair_elements.shape, jnp.bfloat16),
+            pltpu.VMEM(transitions.shape, jnp.int32),
+            pltpu.VMEM(energies.shape, jnp.float32),
+            pltpu.VMEM(occupations.shape, jnp.int32),
+            pltpu.SMEM(frequencies.shape, jnp.float32),
+            dma((5,)), dma, dma((4,)), dma((4,)), dma((64,)), dma((64,)), dma((10,)), dma((10,)), dma((8,)), dma((8,)),
         ],
         compiler_params=pltpu.CompilerParams(
             collective_id=0, has_side_effects=True, vmem_limit_bytes=8 * 2**20
         ),
-    )(pair_elements, transitions, energies.T, occupations.T, frequencies)
+    )(*inputs)
     return pl.pallas_call(
         finish_kernel,
         out_shape=jax.ShapeDtypeStruct((2, 2, width, width), jnp.float32),

time: 58.8 us -> 53.6 us (0.912)
  local copies, waits for them, and re-layouts: 3.88 us -> 0 us
  Pallas kernels: 54.4 us -> 53.2 us
    unnamed x8 -> x0, local copies, waits for them, and re-layouts: 3.88 us -> none
    pallas_call x1, Pallas kernels: 47.9 us -> 46.7 us  [body(): pl.pallas_call(gather_kernel, out_shape=(pltpu.VMEM((4, 2, 4, 4, 16, widt...]
where the time goes in v3:
time: 53.6 us; the launch traced here: 53.3 us
  Pallas kernels  53.2 us (99%)
    pallas_call x1, Pallas kernels, body(): pl.pallas_call(gather_kernel, out_shape=(pltpu.VMEM((4, 2, 4, 4, 16, widt...  46.7 us
    pallas_call x1, Pallas kernels, body(): pl.pallas_call(finish_kernel, out_shape=jax.ShapeDtypeStruct((2, 2, width...  6.45 us

profile of v3, /device:TPU:0, one launch (start us, length us, event | category | flops | bytes accessed | tf_op | source)
XLA Modules:
  0.0 53.3 jit_solution(8051052433932742772)
XLA Ops:
  0.0 46.7 %shard_map.55 = (bf16[4,2,4,4,16,1024]{5,4,3,2,1,0:T(8,128)(2,1)S(1)}, bf16[4,2,4,64,1024]{4,3,2,1,0:T(8,128)(2,1)S(1)}, f32[2,1024]{1,0:T(2,128)S(1)}, f32[2,2,1024,1024]{3,2,1,0:T(8,128)S(1)}) custom-call(bf16[2,64,1024]{2,1,0:T(8,128)(2,1)} %pair_hbm.1, s32[3,1024]{1,0:T(4,128)} %transitions_hbm.1, f32[16,64]{1,0:T(8,128)} %energies_hbm.1, ...), custom_call_target="tpu_custom_call" | custom-call | tf_op jit(solution)/shard_map/pallas_call | solution.py:312
  46.7 6.5 %shard_map.56 = f32[2,2,1024,1024]{3,2,1,0:T(8,128)} custom-call(bf16[4,2,4,4,16,1024]{5,4,3,2,1,0:T(8,128)(2,1)S(1)} %get-tuple-element.9.rowp, bf16[4,2,4,64,1024]{4,3,2,1,0:T(8,128)(2,1)S(1)} %get-tuple-element.10.colp, f32[2,1024]{1,0:T(2,128)S(1)} %get-tuple-element.11.weight, f32[2,2,1024,1024]{3,2,1,0:T(8,128)S(1)} %get-tuple-element.12.total), custom_call_target="tpu_custom_call" | custom-call | tf_op jit(solution)/shard_map/pallas_call | solution.py:334

commit v4 on v3

--- a/solution.py
+++ b/solution.py
@@ -88,12 +88,14 @@
     sent = []
 
     def send(src, dst, sems, slot, there):
+        shared = sems[0] is r_send
         copy = pltpu.make_async_remote_copy(
-            src_ref=src, dst_ref=dst, send_sem=sems[0].at[slot], recv_sem=sems[1].at[slot],
+            src_ref=src, dst_ref=dst, send_sem=sems[0].at[slot // 16 if shared else slot], recv_sem=sems[1].at[slot],
             device_id=there, device_id_type=MESH,
         )
         copy.start()
-        sent.append(copy)
+        if not shared:
+            sent.append(copy)
         return copy
 
     rows, cols, both = (r_send, r_recv), (c_send, c_recv), (b_send, b_recv)
@@ -175,9 +177,9 @@
             go(B3 + 1, ref(1, slice(None), x), to_xm)
         if stage == "a3":
             gather[j, A3].wait_recv()
-            go(A4 + 1, ref(0, s_pair, pl.ds(1, 3)), to_next)
+            go(A4 + 1, ref(0, s_pair, pl.ds(2, 2)), to_next)
             gather[j, A3 + 1].wait_recv()
-            go(A4, ref(0, s_next, pl.ds(0, 1)), to_partner)
+            go(A4, ref(0, s_next, pl.ds(0, 2)), to_partner)
         if stage == "b3":
             gather[j, B3].wait_recv()
             go(B4, ref(1, pl.ds(0, 2), xm), to_xp)
@@ -241,6 +243,12 @@
         waits[index].wait_recv()
     for copy in sent:
         copy.wait_send()
+    for j in range(4):
+        rows_sent = total.at[0, 0, pl.ds(0, 240), :]
+        pltpu.make_async_remote_copy(
+            src_ref=rows_sent, dst_ref=rows_sent, send_sem=r_send.at[j], recv_sem=r_recv.at[0],
+            device_id=to_sibling, device_id_type=MESH,
+        ).wait_send()
     for here, remote in scatter:
         @pl.when(jnp.logical_not(here))
         def _():
@@ -325,7 +333,7 @@
             pltpu.VMEM(energies.shape, jnp.float32),
             pltpu.VMEM(occupations.shape, jnp.int32),
             pltpu.SMEM(frequencies.shape, jnp.float32),
-            dma((5,)), dma, dma((4,)), dma((4,)), dma((64,)), dma((64,)), dma((10,)), dma((10,)), dma((8,)), dma((8,)),
+            dma((5,)), dma, dma((4,)), dma((4,)), dma((4,)), dma((64,)), dma((10,)), dma((10,)), dma((8,)), dma((8,)),
         ],
         compiler_params=pltpu.CompilerParams(
             collective_id=0, has_side_effects=True, vmem_limit_bytes=8 * 2**20

time: 53.6 us -> 52.7 us (0.983)
  Pallas kernels: 53.2 us -> 52.4 us
    pallas_call x1, Pallas kernels: 46.7 us -> 46 us  [body(): pl.pallas_call(gather_kernel, out_shape=(pltpu.VMEM((4, 2, 4, 4, 16, widt...]
where the time goes in v4:
time: 52.7 us; the launch traced here: 52.6 us
  Pallas kernels  52.4 us (99%)
    pallas_call x1, Pallas kernels, body(): pl.pallas_call(gather_kernel, out_shape=(pltpu.VMEM((4, 2, 4, 4, 16, widt...  46 us
    pallas_call x1, Pallas kernels, body(): pl.pallas_call(finish_kernel, out_shape=jax.ShapeDtypeStruct((2, 2, width...  6.46 us

profile of v4, /device:TPU:0, one launch (start us, length us, event | category | flops | bytes accessed | tf_op | source)
XLA Modules:
  0.0 52.6 jit_solution(12125635499785341345)
XLA Ops:
  0.0 46.0 %shard_map.55 = (bf16[4,2,4,4,16,1024]{5,4,3,2,1,0:T(8,128)(2,1)S(1)}, bf16[4,2,4,64,1024]{4,3,2,1,0:T(8,128)(2,1)S(1)}, f32[2,1024]{1,0:T(2,128)S(1)}, f32[2,2,1024,1024]{3,2,1,0:T(8,128)S(1)}) custom-call(bf16[2,64,1024]{2,1,0:T(8,128)(2,1)} %pair_hbm.1, s32[3,1024]{1,0:T(4,128)} %transitions_hbm.1, f32[16,64]{1,0:T(8,128)} %energies_hbm.1, ...), custom_call_target="tpu_custom_call" | custom-call | tf_op jit(solution)/shard_map/pallas_call | solution.py:320
  46.0 6.5 %shard_map.56 = f32[2,2,1024,1024]{3,2,1,0:T(8,128)} custom-call(bf16[4,2,4,4,16,1024]{5,4,3,2,1,0:T(8,128)(2,1)S(1)} %get-tuple-element.9.rowp, bf16[4,2,4,64,1024]{4,3,2,1,0:T(8,128)(2,1)S(1)} %get-tuple-element.10.colp, f32[2,1024]{1,0:T(2,128)S(1)} %get-tuple-element.11.weight, f32[2,2,1024,1024]{3,2,1,0:T(8,128)S(1)} %get-tuple-element.12.total), custom_call_target="tpu_custom_call" | custom-call | tf_op jit(solution)/shard_map/pallas_call | solution.py:342

commit v5 on v4

--- a/solution.py
+++ b/solution.py
@@ -9,7 +9,7 @@
 ORDER = (
     "p0", "z0", "a00", "b00", "p1", "a01", "b01", "a10", "b10", "a02", "b02", "a11", "b11", "a20", "b20", "q0", "q1",
     "a03", "b03", "a12", "b12", "a21", "b21", "a30", "b30", "c1", "a13", "b13", "a22", "b22", "e0", "a31", "b31",
-    "c2", "k0", "a23", "b23", "a32", "b32", "e1", "k1", "a33", "b33", "e2", "c3", "k2", "e3",
+    "c2", "a23", "b23", "k0", "a32", "b32", "e1", "k1", "a33", "b33", "e2", "c3", "k2", "e3",
 )
 
 TILE = 256

time: 52.7 us -> 51.5 us (0.977)
  Pallas kernels: 52.4 us -> 51.2 us
    pallas_call x1, Pallas kernels: 46 us -> 44.7 us  [body(): pl.pallas_call(gather_kernel, out_shape=(pltpu.VMEM((4, 2, 4, 4, 16, widt...]
where the time goes in v5:
time: 51.5 us; the launch traced here: 51.4 us
  Pallas kernels  51.2 us (99%)
    pallas_call x1, Pallas kernels, body(): pl.pallas_call(gather_kernel, out_shape=(pltpu.VMEM((4, 2, 4, 4, 16, widt...  44.7 us
    pallas_call x1, Pallas kernels, body(): pl.pallas_call(finish_kernel, out_shape=jax.ShapeDtypeStruct((2, 2, width...  6.47 us

profile of v5, /device:TPU:0, one launch (start us, length us, event | category | flops | bytes accessed | tf_op | source)
XLA Modules:
  0.0 51.4 jit_solution(11777686222333771665)
XLA Ops:
  0.0 44.7 %shard_map.55 = (bf16[4,2,4,4,16,1024]{5,4,3,2,1,0:T(8,128)(2,1)S(1)}, bf16[4,2,4,64,1024]{4,3,2,1,0:T(8,128)(2,1)S(1)}, f32[2,1024]{1,0:T(2,128)S(1)}, f32[2,2,1024,1024]{3,2,1,0:T(8,128)S(1)}) custom-call(bf16[2,64,1024]{2,1,0:T(8,128)(2,1)} %pair_hbm.1, s32[3,1024]{1,0:T(4,128)} %transitions_hbm.1, f32[16,64]{1,0:T(8,128)} %energies_hbm.1, ...), custom_call_target="tpu_custom_call" | custom-call | tf_op jit(solution)/shard_map/pallas_call | solution.py:320
  44.7 6.5 %shard_map.56 = f32[2,2,1024,1024]{3,2,1,0:T(8,128)} custom-call(bf16[4,2,4,4,16,1024]{5,4,3,2,1,0:T(8,128)(2,1)S(1)} %get-tuple-element.9.rowp, bf16[4,2,4,64,1024]{4,3,2,1,0:T(8,128)(2,1)S(1)} %get-tuple-element.10.colp, f32[2,1024]{1,0:T(2,128)S(1)} %get-tuple-element.11.weight, f32[2,2,1024,1024]{3,2,1,0:T(8,128)S(1)} %get-tuple-element.12.total), custom_call_target="tpu_custom_call" | custom-call | tf_op jit(solution)/shard_map/pallas_call | solution.py:342
